TPU v7x, 32 devices: a whole 2x2x4 slice. The times are simulated.
32 devices in a mesh: groups: 2 (over x), expert: 16 (over z, y, core).
Axes of the slice: x: 2, y: 2, z: 4, core: 2. Of those that a mesh axis runs over, the one named last changes fastest.
Arguments:
- tokens: bfloat16 [256, 7168], P(('groups', 'expert')), parts along dimension 0, may hold values from -6 to 6
- expert_ids: int32 [256, 2], P(('groups', 'expert')), parts along dimension 0, may hold values from 0 to 3, as said below
- gate_scores: float32 [256, 2], P(('groups', 'expert')), parts along dimension 0, may hold values from 0.2 to 1
- w_gate_up: bfloat16 [16, 7168, 512], P('expert'), may hold values from -0.0625 to 0.0625
- w_down: bfloat16 [16, 256, 7168], P('expert'), may hold values from -0.1875 to 0.1875
Outputs:
- moe_out: bfloat16 [256, 7168], P(('groups', 'expert')), parts along dimension 0
There are 2 independent parts, one for each index of `groups`. A program takes and returns all parts, laid end to end along the dimension named above; an argument that names none is the same for every part. Nothing has to cross between parts.
Inputs may be any that keep to these rules, and one draw needn't show every extreme that they name: `expert_ids`: each row names 2 different experts. In each aligned block of 8 rows (the rows of one device) no expert is named by more than 8 rows, and one expert is named by exactly 8 rows in every block.
All inputs are finite; a program needn't handle non-finite values.
Results may differ from a plain program's by a relative error of at most 0.0058.
Values may be sent and summed in bfloat16 or wider, within the bound.
A program may use at most 128 MiB of HBM per device.

v0:
```python
import jax
import jax.numpy as jnp
from jax import lax
from jax.sharding import PartitionSpec as P

SPLIT = 4


route_scale = 2.5


def expert_block(block_tokens, gate_up_part, down_part):
    hidden_width = down_part.shape[0]
    gate_up = jnp.dot(block_tokens, gate_up_part, preferred_element_type=jnp.float32)
    hidden = (jax.nn.silu(gate_up[:, :hidden_width]) * gate_up[:, hidden_width:]).astype(
        jnp.bfloat16
    )
    return jnp.dot(hidden, down_part, preferred_element_type=jnp.float32).astype(jnp.bfloat16)


def rank_within(values_in, class_count):
    one_hot = (values_in[:, None] == jnp.arange(class_count, dtype=jnp.int32)[None, :]).astype(
        jnp.int32
    )
    earlier = jnp.cumsum(one_hot, axis=0) - one_hot
    return jnp.sum(earlier * one_hot, axis=1)


def serve(flat_rows, flat_labels, label_value, gate_up_part, down_part, results):
    finished = expert_block(flat_rows, gate_up_part, down_part)
    served_rows = jnp.where((flat_labels == label_value)[:, None], finished, results)
    return served_rows


def body(tokens, expert_ids, gate_scores, w_gate_up, w_down):
    dev_count = lax.axis_size("expert")
    rows_dev = expert_ids.shape[0]
    route_count = expert_ids.shape[1]
    model_width = tokens.shape[1]
    expert_count = dev_count // SPLIT
    slot_count = 2 * rows_dev * route_count // expert_count
    group_slots = expert_count * slot_count
    slot_total = dev_count * slot_count
    weights = route_scale * gate_scores / jnp.sum(gate_scores, axis=1, keepdims=True)
    flat_ids = expert_ids.reshape(-1)
    home_gate_up = w_gate_up[0]
    home_down = w_down[0]
    route_label = jnp.zeros_like(flat_ids)
    served = ((0, home_gate_up, home_down),)
    rank = rank_within(flat_ids, expert_count)
    target = flat_ids * slot_count + rank
    route_rows = jnp.arange(rows_dev * route_count, dtype=jnp.int32) // route_count
    source_of = jnp.full((group_slots,), rows_dev, jnp.int32).at[target].set(route_rows)
    label_of = jnp.full((group_slots,), -1, jnp.int32).at[target].set(route_label)
    outgoing = jnp.take(tokens, source_of, axis=0, mode="fill", fill_value=0)
    outgoing = jnp.broadcast_to(
        outgoing.reshape(expert_count, 1, slot_count, model_width),
        (expert_count, SPLIT, slot_count, model_width),
    ).reshape(dev_count, slot_count, model_width)
    label_out = jnp.broadcast_to(
        label_of.reshape(expert_count, 1, slot_count), (expert_count, SPLIT, slot_count)
    ).reshape(dev_count, slot_count)
    arrived, labels = (
        lax.all_to_all(outgoing, "expert", split_axis=0, concat_axis=0, tiled=True),
        lax.all_to_all(label_out, "expert", split_axis=0, concat_axis=0, tiled=True),
    )
    flat_rows = arrived.reshape(slot_total, model_width)
    flat_labels = labels.reshape(slot_total)
    results = jnp.zeros((slot_total, model_width), jnp.bfloat16)
    label_value, gate_up_part, down_part = served[0]
    results = serve(flat_rows, flat_labels, label_value, gate_up_part, down_part, results)
    returned = lax.all_to_all(
        results.reshape(dev_count, slot_count, model_width),
        "expert",
        split_axis=0,
        concat_axis=0,
        tiled=True,
    )
    grouped = returned.reshape(expert_count, SPLIT, slot_count, model_width)
    picked = grouped[flat_ids, :, rank]
    expert_out = jnp.sum(picked.astype(jnp.float32), axis=1).reshape(
        rows_dev, route_count, model_width
    )
    combined = jnp.sum(weights[:, :, None] * expert_out, axis=1)
    return combined.astype(jnp.bfloat16)


def solution(mesh):
    in_specs = (
        P(("groups", "expert"), None),
        P(("groups", "expert"), None),
        P(("groups", "expert"), None),
        P("expert", None, None),
        P("expert", None, None),
    )
    out_specs = P(("groups", "expert"), None)
    return jax.shard_map(body, mesh=mesh, in_specs=in_specs, out_specs=out_specs, check_vma=False)
```

profile of v0, /device:TPU:13, one launch (start us, length us, event | category | flops | bytes accessed | tf_op | source)
XLA Modules:
  0.0 123.6 jit_solution(11272302360567906375)
XLA Ops:
  0.0 0.0 copy-start
  0.0 0.8 copy.26
  0.8 0.1 eq.28
  0.9 0.1 reshape.121
  1.0 0.1 fusion.9
  1.1 0.2 select_reduce_fusion
  1.3 0.6 scatter_custom_fusion
  1.9 0.1 broadcast_in_dim.52
  2.0 0.6 broadcast_in_dim.53
  2.6 6.5 %all-to-all-start = ((s32[16,1,8]{2,1,0:T(1,128)}), s32[16,1,8]{2,1,0:T(1,128)S(1)}, u32[]{:S(2)}, u32[]{:S(2)}) async-start(s32[16,1,8]{2,1,0:T(1,128)} %bitcast.3), calls=%async_computation | async-start | bytes 16384 | tf_op jit(solution)/shard_map/all_to_all | solution.py:65
  9.1 0.6 scatter_custom_fusion.1
  9.8 0.1 broadcast_in_dim.56
  9.9 0.0 copy-done
  9.9 0.8 gather_fusion
  10.7 0.1 bitcast_select_fusion
  10.8 2.1 %all-to-all-done = s32[16,1,8]{2,1,0:T(1,128)S(1)} async-done(((s32[16,1,8]{2,1,0:T(1,128)}), s32[16,1,8]{2,1,0:T(1,128)S(1)}, u32[]{:S(2)}, u32[]{:S(2)}) %all-to-all-start) | async-done | bytes 544 | tf_op jit(solution)/shard_map/all_to_all | solution.py:65
  12.9 1.4 %broadcast_in_dim.60 = bf16[4,4,8,7168]{3,2,1,0:T(8,128)(2,1)} broadcast(bf16[4,8,7168]{2,1,0:T(8,128)(2,1)S(1)} %bitcast_select_fusion), dimensions={0,2,3} | broadcast | bytes 2293760 | tf_op jit(solution)/shard_map/broadcast_in_dim | solution.py:56
  14.3 6.2 %all-to-all-start.1 = ((bf16[16,8,7168]{2,1,0:T(8,128)(2,1)}), bf16[16,8,7168]{2,1,0:T(8,128)(2,1)S(1)}, u32[]{:S(2)}, u32[]{:S(2)}) async-start(bf16[16,8,7168]{2,1,0:T(8,128)(2,1)} %bitcast.30), calls=%async_computation.1 | async-start | bytes 3670016 | tf_op jit(solution)/shard_map/all_to_all | solution.py:64
  20.6 0.1 eq.34
  20.7 41.7 %all-to-all-done.1 = bf16[16,8,7168]{2,1,0:T(8,128)(2,1)S(1)} async-done(((bf16[16,8,7168]{2,1,0:T(8,128)(2,1)}), bf16[16,8,7168]{2,1,0:T(8,128)(2,1)S(1)}, u32[]{:S(2)}, u32[]{:S(2)}) %all-to-all-start.1) | async-done | bytes 1835040 | tf_op jit(solution)/shard_map/all_to_all | solution.py:64
  62.4 0.0 copy-start.1
  62.4 4.3 %fusion.2 = f32[128,512]{1,0:T(8,128)S(1)} fusion(bf16[1,7168,512]{2,1,0:T(8,128)(2,1)} %param.8, bf16[16,8,7168]{2,1,0:T(8,128)(2,1)S(1)} %all-to-all-done.1), kind=kOutput, calls=%fused_computation.7 | convolution fusion | flops 939524096 | bytes 9437184 | tf_op jit(solution)/shard_map/dot_general | solution.py:14
  66.7 0.0 copy-done.1
  66.7 1.9 %fusion.1 = bf16[16,8,7168]{2,1,0:T(8,128)(2,1)} fusion(bf16[1,256,7168]{2,1,0:T(8,128)(2,1)S(1)} %copy-done.1, pred[128]{0:T(512)(128)(4,1)S(1)} %eq.34, f32[128,512]{1,0:T(8,128)S(1)} %fusion.2), kind=kOutput, calls=%fused_computation.6 | convolution fusion | flops 471793664 | bytes 5767296 | tf_op jit(solution)/shard_map/dot_general | solution.py:18
  68.7 0.0 copy-start.2
  68.7 4.9 %all-to-all-start.2 = ((bf16[16,8,7168]{2,1,0:T(8,128)(2,1)}), bf16[16,8,7168]{2,1,0:T(8,128)(2,1)S(1)}, u32[]{:S(2)}, u32[]{:S(2)}) async-start(bf16[16,8,7168]{2,1,0:T(8,128)(2,1)} %fusion.1), calls=%async_computation.2 | async-start | bytes 3670016 | tf_op jit(solution)/shard_map/all_to_all | solution.py:72
  73.6 0.0 copy-done.2
  73.6 0.1 copy.25
  73.7 41.7 %all-to-all-done.2 = bf16[16,8,7168]{2,1,0:T(8,128)(2,1)S(1)} async-done(((bf16[16,8,7168]{2,1,0:T(8,128)(2,1)}), bf16[16,8,7168]{2,1,0:T(8,128)(2,1)S(1)}, u32[]{:S(2)}, u32[]{:S(2)}) %all-to-all-start.2) | async-done | bytes 1835040 | tf_op jit(solution)/shard_map/all_to_all | solution.py:72
  115.4 2.7 %copy.29 = bf16[4,4,8,7168]{3,1,2,0:T(4,128)(2,1)} copy(bf16[4,4,8,7168]{3,2,1,0:T(8,128)(2,1)S(1)} %bitcast.29) | data formatting | bytes 3670016 | tf_op jit(solution)/shard_map/reshape | solution.py:79
  118.0 2.8 %gather_fusion.1 = bf16[16,4,7168]{2,1,0:T(4,128)(2,1)S(1)} fusion(bf16[4,4,8,7168]{3,1,2,0:T(4,128)(2,1)} %copy.29, s32[16]{0:T(128)S(1)} %get-tuple-element.5), kind=kCustom, calls=%fused_computation.1 | custom fusion | bytes 1835136 | tf_op jit(solution)/shard_map/gather | solution.py:80
  120.9 1.2 convert_reduce_fusion
  122.1 0.3 reshape.126
  122.3 1.3 %multiply_reduce_fusion = bf16[8,7168]{1,0:T(8,128)(2,1)} fusion(f32[8,2,7168]{2,1,0:T(2,128)S(1)} %reshape.126, f32[8,2]{1,0:T(8,128)S(1)} %copy.25), kind=kLoop, calls=%fused_computation.13 | loop fusion | flops 172032 | bytes 573504 | tf_op jit(solution)/shard_map/reduce_sum | solution.py:84
  (10 shorter events, 0.1 us)
Async XLA Ops:
  0.0 9.9 %copy-start = (bf16[8,7168]{1,0:T(8,128)(2,1)S(1)}, bf16[8,7168]{1,0:T(8,128)(2,1)}, u32[]{:S(2)}) copy-start(bf16[8,7168]{1,0:T(8,128)(2,1)} %param.5) | copy-start | bytes 344068
  2.6 10.3 %all-to-all-start = ((s32[16,1,8]{2,1,0:T(1,128)}), s32[16,1,8]{2,1,0:T(1,128)S(1)}, u32[]{:S(2)}, u32[]{:S(2)}) async-start(s32[16,1,8]{2,1,0:T(1,128)} %bitcast.3), calls=%async_computation | async-start | bytes 16384 | tf_op jit(solution)/shard_map/all_to_all | solution.py:65
  14.3 48.0 %all-to-all-start.1 = ((bf16[16,8,7168]{2,1,0:T(8,128)(2,1)}), bf16[16,8,7168]{2,1,0:T(8,128)(2,1)S(1)}, u32[]{:S(2)}, u32[]{:S(2)}) async-start(bf16[16,8,7168]{2,1,0:T(8,128)(2,1)} %bitcast.30), calls=%async_computation.1 | async-start | bytes 3670016 | tf_op jit(solution)/shard_map/all_to_all | solution.py:64
  62.4 4.4 %copy-start.1 = (bf16[1,256,7168]{2,1,0:T(8,128)(2,1)S(1)}, bf16[1,256,7168]{2,1,0:T(8,128)(2,1)}, u32[]{:S(2)}) copy-start(bf16[1,256,7168]{2,1,0:T(8,128)(2,1)} %param.9) | copy-start | bytes 11010052
  68.7 4.9 %copy-start.2 = (f32[8,2]{0,1:T(2,128)S(1)}, f32[8,2]{0,1:T(2,128)}, u32[]{:S(2)}) copy-start(f32[8,2]{0,1:T(2,128)} %param.7) | copy-start | bytes 196
  68.7 46.7 %all-to-all-start.2 = ((bf16[16,8,7168]{2,1,0:T(8,128)(2,1)}), bf16[16,8,7168]{2,1,0:T(8,128)(2,1)S(1)}, u32[]{:S(2)}, u32[]{:S(2)}) async-start(bf16[16,8,7168]{2,1,0:T(8,128)(2,1)} %fusion.1), calls=%async_computation.2 | async-start | bytes 3670016 | tf_op jit(solution)/shard_map/all_to_all | solution.py:72
where the time goes:
time: 124 us
  waiting for transfers between devices  85.4 us (69%)
  starting transfers between devices  17.6 us (14%)
  local copies, waits for them, and re-layouts  11.2 us (9%)
  matrix products  6.28 us (5%)
  other arithmetic  2.96 us (2%)
    all_to_all x1, waiting for transfers between devices, body(): lax.all_to_all(outgoing, 'expert', split_axis=0, concat_axis=0, tiled=True)  41.7 us
    all_to_all x1, waiting for transfers between devices, body(): lax.all_to_all(results.reshape(dev_count, slot_count, model_width), 'expe...  41.7 us
    all_to_all x1, starting transfers between devices, body(): lax.all_to_all(label_out, 'expert', split_axis=0, concat_axis=0, tiled=True)  6.52 us
    all_to_all x1, starting transfers between devices, body(): lax.all_to_all(outgoing, 'expert', split_axis=0, concat_axis=0, tiled=True)  6.21 us
    all_to_all x1, starting transfers between devices, body(): lax.all_to_all(results.reshape(dev_count, slot_count, model_width), 'expe...  4.9 us
    dot_general x1, matrix products, expert_block(): jnp.dot(block_tokens, gate_up_part, preferred_element_type=jnp.float32)  4.35 us
    gather x1, local copies, waits for them, and re-layouts, body(): picked = grouped[flat_ids, :, rank]  2.83 us
    reshape x1, local copies, waits for them, and re-layouts, body(): grouped = returned.reshape(expert_count, SPLIT, slot_count, model_width)  2.67 us
  transfers between devices with their start and end apart: 3, of which 3 were waited for; matrix products, arithmetic and copies ran while one was open for 2% of the time, Pallas kernels for 0%

commit v1 on v0

v1 whole, which is shorter than its diff:
```python
import functools
import jax
import jax.numpy as jnp
from jax import lax
from jax.experimental import pallas as pl
from jax.experimental.pallas import tpu as pltpu
from jax.sharding import PartitionSpec as P

SPLIT = 4
ROUTE_SCALE = 2.5
W1_PIECES = 4
W2_PIECES = 2
BF16 = jnp.bfloat16
F32 = jnp.float32


def kernel(planes, down_cols, tok_ref, ids_ref, score_ref, w1_hbm, w2_hbm, out_ref,
           x, s, w1, w2, part, r1, ysend, r2, zsend, r3, own,
           snd, rcv, wsem, tsem):
    rows, width = tok_ref.shape
    hidden_width = w2.shape[0]
    me = lax.axis_index("expert")
    p = me // SPLIT
    q = me % SPLIT
    y = q // 2
    c = q % 2
    ypeer = p * SPLIT + (1 - y) * 2 + c
    cpeer = p * SPLIT + y * 2 + (1 - c)
    qy = (1 - y) * 2 + c

    tok_copy = pltpu.make_async_copy(tok_ref, x.at[p, q], tsem)
    tok_copy.start()
    depth1 = w1.shape[0] // W1_PIECES
    depth2 = w2.shape[0] // W2_PIECES
    w1_copies = [
        pltpu.make_async_copy(w1_hbm.at[0, pl.ds(i * depth1, depth1)],
                              w1.at[pl.ds(i * depth1, depth1)], wsem.at[i])
        for i in range(W1_PIECES)
    ]
    w2_copies = [
        pltpu.make_async_copy(w2_hbm.at[0, pl.ds(i * depth2, depth2)],
                              w2.at[pl.ds(i * depth2, depth2)], wsem.at[W1_PIECES + i])
        for i in range(W2_PIECES)
    ]

    barrier = pltpu.get_barrier_semaphore()

    def greet(idx):
        pl.semaphore_signal(barrier, inc=1, device_id={"expert": idx},
                            device_id_type=pl.DeviceIdType.MESH)

    greet(cpeer)
    greet(ypeer)

    @pl.when(p > 0)
    def _():
        greet(me - SPLIT)

    @pl.when(p < planes - 1)
    def _():
        greet(me + SPLIT)

    for cp in w1_copies + w2_copies:
        cp.start()

    scores = score_ref[...]
    weights = ROUTE_SCALE * scores / jnp.sum(scores, axis=1, keepdims=True)
    lanes = s.shape[-1]
    lane = lax.broadcasted_iota(jnp.int32, (rows, lanes), 1)
    row = lax.broadcasted_iota(jnp.int32, (rows, lanes), 0)
    table = jnp.zeros((rows, lanes), F32)
    for k in range(ids_ref.shape[1]):
        table = table + jnp.where(lane == ids_ref[:, k:k + 1] * rows + row,
                                  weights[:, k:k + 1], 0.0)
    s[p, q] = jnp.sum(table, axis=0, keepdims=True)

    tok_copy.wait()
    neighbours = (2 + jnp.where(p > 0, 1, 0) + jnp.where(p < planes - 1, 1, 0)).astype(jnp.int32)
    pl.semaphore_wait(barrier, neighbours)

    def remote(src, dst, kind, rkind, plane, rplane, target):
        return pltpu.make_async_remote_copy(
            src_ref=src, dst_ref=dst, send_sem=snd.at[kind, plane],
            recv_sem=rcv.at[rkind, rplane], device_id={"expert": target},
            device_id_type=pl.DeviceIdType.MESH)

    def gather_copy(kind, plane):
        col = qy if kind == 4 else q
        target = (me + SPLIT, me - SPLIT, ypeer, cpeer, cpeer)[kind]
        rkind = 0 if kind == 1 else kind
        return (
            remote(x.at[plane, col], x.at[plane, col], kind, rkind, plane, plane, target),
            remote(s.at[plane, col], s.at[plane, col], kind + 5, rkind + 5, plane, plane, target),
        )

    def start(kind, plane):
        for cp in gather_copy(kind, plane):
            cp.start()

    def wait_recv(kind, plane):
        for cp in gather_copy(kind, plane):
            cp.wait_recv()

    def wait_send(kind, plane):
        for cp in gather_copy(kind, plane):
            cp.wait_send()

    low = jnp.minimum(p, planes - 1 - p)

    def plane_of(t):
        near = (t + 1) // 2
        alt = jnp.where(t % 2 == 1, p - near, p + near)
        far = t - low
        tail = jnp.where(p < planes - 1 - p, p + far, p - far)
        return jnp.where(t <= 2 * low, alt, tail)

    def goes_up(plane):
        return jnp.logical_and(plane <= p, p < planes - 1)

    def goes_down(plane):
        return jnp.logical_and(plane >= p, p > 0)

    def stage_a(t):
        plane = plane_of(t)

        @pl.when(plane != p)
        def _():
            wait_recv(0, plane)

        @pl.when(goes_up(plane))
        def _():
            start(0, plane)

        @pl.when(goes_down(plane))
        def _():
            start(1, plane)

        start(2, plane)
        start(3, plane)

    def stage_b(t):
        plane = plane_of(t)
        wait_recv(2, plane)
        start(4, plane)

    def core_copy(plane):
        return remote(part.at[plane, 1 - c], r1.at[plane], 10, 10, plane, plane, cpeer)

    def y_copy(plane):
        return remote(ysend.at[plane], r2.at[plane], 11, 11, plane, plane, ypeer)

    def z_copy(plane):
        return remote(zsend.at[plane], r3.at[p], 12, 12, plane, p, plane * SPLIT + q)

    def stage_c(t):
        plane = plane_of(t)
        wait_recv(3, plane)
        wait_recv(4, plane)
        block = x[plane].reshape(SPLIT * rows, width)
        gate_up = jnp.dot(block, w1[...], preferred_element_type=F32)
        gate = gate_up[:, :hidden_width]
        hidden = (gate / (1.0 + jnp.exp(-gate)) * gate_up[:, hidden_width:]).astype(BF16)
        chunk_s = jnp.broadcast_to(s[plane], (SPLIT, rows, lanes))
        lane3 = lax.broadcasted_iota(jnp.int32, (SPLIT, rows, lanes), 2)
        row3 = lax.broadcasted_iota(jnp.int32, (SPLIT, rows, lanes), 1)
        scale = jnp.sum(jnp.where(lane3 == p * rows + row3, chunk_s, 0.0), axis=2, keepdims=True)
        scale = scale.reshape(SPLIT * rows, 1)
        for j in range(width // down_cols):
            cols = pl.ds(j * down_cols, down_cols)
            res = jnp.dot(hidden, w2[:, cols], preferred_element_type=F32) * scale
            res = res.astype(BF16)
            for b in range(SPLIT):
                part[plane, b % 2, b // 2, :, cols] = res[b * rows:(b + 1) * rows]
        core_copy(plane).start()

    def stage_d(t):
        plane = plane_of(t)
        core_copy(plane).wait_recv()
        ysend[plane] = (part[plane, c, 1 - y].astype(F32)
                        + r1[plane, 1 - y].astype(F32)).astype(BF16)
        y_copy(plane).start()

    def stage_e(t):
        plane = plane_of(t)
        y_copy(plane).wait_recv()
        total = (part[plane, c, y].astype(F32) + r1[plane, y].astype(F32)
                 + r2[plane].astype(F32))

        @pl.when(plane == p)
        def _():
            own[...] = total

        @pl.when(plane != p)
        def _():
            zsend[plane] = total.astype(BF16)
            z_copy(plane).start()

    stage_a(0)
    stage_a(1)
    stage_b(0)
    for cp in w1_copies + w2_copies:
        cp.wait()

    def step(i, carry):
        stage_c(i)

        @pl.when(i + 2 < planes)
        def _():
            stage_a(i + 2)

        @pl.when(i + 1 < planes)
        def _():
            stage_b(i + 1)

        @pl.when(i > 0)
        def _():
            stage_e(i - 1)

        stage_d(i)
        return carry

    lax.fori_loop(0, planes, step, 0)
    stage_e(planes - 1)

    def drain(plane, carry):
        @pl.when(goes_up(plane))
        def _():
            wait_send(0, plane)

        @pl.when(goes_down(plane))
        def _():
            wait_send(1, plane)

        for kind in (2, 3, 4):
            wait_send(kind, plane)
        core_copy(plane).wait_send()
        y_copy(plane).wait_send()
        return carry

    lax.fori_loop(0, planes, drain, 0)

    def collect(k, carry):
        plane = lax.rem(p + k, planes)
        remote(zsend.at[plane], r3.at[plane], 12, 12, plane, plane, plane * SPLIT + q).wait()
        own[...] += r3[plane].astype(F32)
        return carry

    lax.fori_loop(1, planes, collect, 0)
    out_ref[...] = own[...].astype(BF16)


def body(tokens, expert_ids, gate_scores, w_gate_up, w_down):
    dev_count = lax.axis_size("expert")
    planes = dev_count // SPLIT
    rows, width = tokens.shape
    hidden_width = w_down.shape[1]
    lanes = -(-planes * rows // 128) * 128
    down_cols = 1024 if width % 1024 == 0 else 128
    blk = (rows, width)
    vmem = pl.BlockSpec(memory_space=pltpu.VMEM)
    hbm = pl.BlockSpec(memory_space=pl.ANY)
    return pl.pallas_call(
        functools.partial(kernel, planes, down_cols),
        out_shape=jax.ShapeDtypeStruct(blk, BF16),
        in_specs=[hbm, vmem, vmem, hbm, hbm],
        out_specs=vmem,
        scratch_shapes=[
            pltpu.VMEM((planes, SPLIT) + blk, BF16),
            pltpu.VMEM((planes, SPLIT, 1, lanes), F32),
            pltpu.VMEM((width, 2 * hidden_width), BF16),
            pltpu.VMEM((hidden_width, width), BF16),
            pltpu.VMEM((planes, 2, 2) + blk, BF16),
            pltpu.VMEM((planes, 2) + blk, BF16),
            pltpu.VMEM((planes,) + blk, BF16),
            pltpu.VMEM((planes,) + blk, BF16),
            pltpu.VMEM((planes,) + blk, BF16),
            pltpu.VMEM((planes,) + blk, BF16),
            pltpu.VMEM(blk, F32),
            pltpu.SemaphoreType.DMA((13, planes)),
            pltpu.SemaphoreType.DMA((13, planes)),
            pltpu.SemaphoreType.DMA((W1_PIECES + W2_PIECES,)),
            pltpu.SemaphoreType.DMA,
        ],
        compiler_params=pltpu.CompilerParams(
            collective_id=0, has_side_effects=True, vmem_limit_bytes=63 * 1024 * 1024),
        name="expert_layer",
    )(tokens, expert_ids, gate_scores, w_gate_up, w_down)


def solution(mesh):
    rows = P(("groups", "expert"), None)
    weights = P("expert", None, None)
    return jax.shard_map(body, mesh=mesh, in_specs=(rows, rows, rows, weights, weights),
                         out_specs=rows, check_vma=False)
```

time: 124 us -> 46 us (0.37)
  the two profiles are of different devices: /device:TPU:13 before, /device:TPU:0 now
where the time goes in v1:
time: 46 us; the launch traced here: 45.7 us
  Pallas kernels  41.5 us (90%)
  local copies, waits for them, and re-layouts  4.24 us (9%)
    pallas_call x1, Pallas kernels, body(): pl.pallas_call(functools.partial(kernel, planes, down_cols), out_shape=ja...  41.5 us
    unnamed x3, local copies, waits for them, and re-layouts  4.24 us

profile of v1, /device:TPU:0, one launch (start us, length us, event | category | flops | bytes accessed | tf_op | source)
XLA Modules:
  0.0 45.7 jit_solution(948022457014743268)
XLA Ops:
  0.0 1.3 %copy.6.ids_ref = s32[8,2]{1,0:T(8,128)} copy(s32[8,2]{0,1:T(2,128)} %param.6) | data formatting | bytes 128 | tf_op args[1]
  1.3 1.3 %copy.7.score_ref = f32[8,2]{1,0:T(8,128)} copy(f32[8,2]{0,1:T(2,128)} %param.7) | data formatting | bytes 128 | tf_op args[2]
  2.7 41.5 %expert_layer.1 = bf16[8,7168]{1,0:T(8,128)(2,1)} custom-call(bf16[8,7168]{1,0:T(8,128)(2,1)} %tok_ref.1, s32[8,2]{1,0:T(8,128)} %copy.6.ids_ref, f32[8,2]{1,0:T(8,128)} %copy.7.score_ref, bf16[1,7168,512]{2,1,0:T(8,128)(2,1)} %w1_hbm.1, bf16[1,256,7168]{2,1,0:T(8,128)(2,1)} %w2_hbm.1), custom_call_target="tpu_custom_call" | custom-call | tf_op jit(solution)/shard_map/expert_layer/pallas_call | solution.py:262
  44.2 1.6 %copy.9 = bf16[8,7168]{1,0:T(8,128)(2,1)} copy(bf16[8,7168]{1,0:T(8,128)(2,1)} %expert_layer.1) | data formatting | bytes 229376
